TPU v7x, 128 devices: a whole 4x4x4 slice. The times are simulated.
128 devices in a mesh: req: 16 (over z, y), mlp: 8 (over x, core).
Axes of the slice: x: 4, y: 4, z: 4, core: 2. Of those that a mesh axis runs over, the one named last changes fastest.
Arguments:
- activations: bfloat16 [8192, 4096], P('req', 'mlp')
- slot_segment: int32 [8192], P('req'), may hold values from -1 to 511, as said below
- attn_norm_gain: float32 [4096], replicated, may hold values from 0.5 to 1.5
- attn_norm_bias: float32 [4096], replicated, may hold values from -1.5 to 1.5
- mlp_norm_gain: float32 [4096], replicated, may hold values from 0.5 to 1.5
- mlp_norm_bias: float32 [4096], replicated, may hold values from -1.5 to 1.5
- qkv_weight: bfloat16 [4096, 6144], P(None, 'mlp')
- dense_weight: bfloat16 [2048, 4096], P('mlp'), may hold values from -0.1875 to 0.1875
- fc_weight: bfloat16 [4096, 8192], P(None, 'mlp'), may hold values from -0.09375 to 0.09375
- proj_weight: bfloat16 [8192, 4096], P('mlp'), may hold values from -0.09375 to 0.09375
Outputs:
- output_rows: float32 [8192, 4096], P('req', 'mlp')
- cache_rows: bfloat16 [2, 4096, 2048], P(None, 'req', 'mlp')
Inputs may be any that keep to these rules, and one draw needn't show every extreme that they name: `slot_segment`: each group's 512 slots hold live slots first and -1 after them; the live count of every group is a multiple of 16 between 16 and 512, the counts of all groups sum to 4096, and some group is full, its last slot beginning a prompt of one token. A live slot holds the group slot where its prompt begins; a prompt's slots are consecutive.
All inputs are finite; a program needn't handle non-finite values.
Results may differ from a plain program's by a relative error of at most 0.0047.
The roundings to bfloat16 on the way count: a program that leaves them out, or rounds other values in their place, can miss the bound.
Values may be sent and summed in bfloat16 or wider, within the bound.
A program may use at most 128 MiB of HBM per device.

v0:
```python
import jax
import jax.numpy as jnp
from jax import lax
from jax.sharding import PartitionSpec as P

HD = 128
ROT = 32
LIVE_DEV = 256


def layer_norm(row_data, gain_vec, bias_vec):
    row_data = row_data.astype(jnp.float32)
    row_mean = jnp.mean(row_data, axis=-1, keepdims=True)
    centered = row_data - row_mean
    variance = jnp.mean(centered * centered, axis=-1, keepdims=True)
    return (centered * lax.rsqrt(variance + 1e-05) * gain_vec + bias_vec).astype(jnp.bfloat16)


def rotate(head_data, position):
    half_rot = ROT // 2
    inv_freq = 10000.0 ** (-(jnp.arange(half_rot).astype(jnp.float32) * 2.0 / ROT))
    angles = position.astype(jnp.float32)[:, None] * inv_freq[None, :]
    cosine = jnp.concatenate([jnp.cos(angles), jnp.cos(angles)], axis=-1)[:, None, :]
    sine_part = jnp.concatenate([jnp.sin(angles), jnp.sin(angles)], axis=-1)[:, None, :]
    rot_part = head_data[..., :ROT]
    pass_part = head_data[..., ROT:]
    first_half = rot_part[..., :half_rot]
    second = rot_part[..., half_rot:]
    turned = jnp.concatenate([-second, first_half], axis=-1)
    return jnp.concatenate([rot_part * cosine + turned * sine_part, pass_part], axis=-1)


def attend(normed, segment, qkv_weight):
    slot_count = normed.shape[0]
    head_count = qkv_weight.shape[1] // (3 * HD)
    mixed_proj = jnp.dot(normed, qkv_weight, preferred_element_type=jnp.float32).reshape(
        slot_count, head_count, 3, HD
    )
    slot_index = jnp.arange(slot_count, dtype=jnp.int32)
    position = slot_index - segment
    query_rows = rotate(mixed_proj[:, :, 0], position).astype(jnp.bfloat16)
    key_rows = rotate(mixed_proj[:, :, 1], position).astype(jnp.bfloat16)
    value_rows = mixed_proj[:, :, 2].astype(jnp.bfloat16)
    scores = jnp.einsum(
        "qhd,khd->hqk", query_rows, key_rows, preferred_element_type=jnp.float32
    ) * HD ** (-0.5)
    allowed = (
        (segment[:, None] == segment[None, :])
        & (slot_index[None, :] <= slot_index[:, None])
        & (segment[:, None] >= 0)
    )
    scores = jnp.where(allowed[None], scores, -1e30)
    row_max = jnp.max(scores, axis=-1, keepdims=True)
    weights = jnp.exp(scores - row_max)
    prob_rows = (weights / jnp.sum(weights, axis=-1, keepdims=True)).astype(jnp.bfloat16)
    context = jnp.einsum("hqk,khd->qhd", prob_rows, value_rows, preferred_element_type=jnp.float32)
    context = context.astype(jnp.bfloat16).reshape(slot_count, head_count * HD)
    return (
        context,
        key_rows.reshape(slot_count, head_count * HD),
        value_rows.reshape(slot_count, head_count * HD),
    )


def body(
    activations,
    slot_segment,
    attn_norm_gain,
    attn_norm_bias,
    mlp_norm_gain,
    mlp_norm_bias,
    qkv_weight,
    dense_weight,
    fc_weight,
    proj_weight,
):
    slot_count = activations.shape[0]
    groups = lax.axis_size("req")
    per_peer = slot_count // groups
    live_slot = slot_segment >= 0
    group_fill = lax.all_gather(
        jnp.sum(live_slot.astype(jnp.int32)).reshape(1), "req", axis=0, tiled=True
    )
    group_units = group_fill // groups
    received_live = (jnp.arange(per_peer, dtype=jnp.int32)[None, :] < group_units[:, None]).reshape(
        -1
    )
    live_rank = jnp.cumsum(received_live.astype(jnp.int32)) - 1
    target = jnp.where(received_live, live_rank, LIVE_DEV)
    pick_rows = (
        jnp.zeros((LIVE_DEV,), jnp.int32)
        .at[target]
        .set(jnp.arange(groups * per_peer, dtype=jnp.int32), mode="drop")
    )
    full_rows = lax.all_gather(activations, "mlp", axis=1, tiled=True)
    normed = layer_norm(full_rows, attn_norm_gain, attn_norm_bias)
    context, key_rows, value_rows = attend(normed, slot_segment, qkv_weight)
    key_value = jnp.concatenate([key_rows, value_rows], axis=1).reshape(per_peer, groups, -1)
    cache_rows = lax.all_to_all(key_value, "req", split_axis=1, concat_axis=0, tiled=True)
    cache_rows = jnp.take(cache_rows.reshape(groups * per_peer, -1), pick_rows, axis=0)
    width = key_rows.shape[1]
    cache_rows = jnp.stack([cache_rows[:, :width], cache_rows[:, width:]])
    mlp_normed = layer_norm(full_rows, mlp_norm_gain, mlp_norm_bias)
    hidden = jax.nn.gelu(
        jnp.dot(mlp_normed, fc_weight, preferred_element_type=jnp.float32), approximate=False
    )
    hidden = hidden.astype(jnp.bfloat16)
    part = jnp.dot(context, dense_weight, preferred_element_type=jnp.float32) + jnp.dot(
        hidden, proj_weight, preferred_element_type=jnp.float32
    )
    total = lax.psum_scatter(
        part.astype(jnp.bfloat16), "mlp", scatter_dimension=1, tiled=True
    ).astype(jnp.float32)
    combined = activations.astype(jnp.float32) + total
    output_rows = jnp.where(live_slot[:, None], combined, 0.0)
    return (output_rows, cache_rows)


def solution(mesh):
    placed = (
        P("req", "mlp"),
        P("req"),
        P(),
        P(),
        P(),
        P(),
        P(None, "mlp"),
        P("mlp", None),
        P(None, "mlp"),
        P("mlp", None),
    )
    return jax.shard_map(
        body,
        mesh=mesh,
        in_specs=placed,
        out_specs=(P("req", "mlp"), P(None, "req", "mlp")),
        check_vma=False,
    )
```

profile of v0, /device:TPU:0, one launch (start us, length us, event | category | flops | bytes accessed | tf_op | source)
XLA Modules:
  0.0 147.7 jit_solution(17991416886373539449)
XLA Ops:
  8.0 1.3 convert_reduce_fusion.1
  10.5 1.0 fusion.71
  11.5 1.0 copy.46
  12.6 31.7 %all-gather.2.cloned.1.call-done = bf16[512,4096]{1,0:T(8,128)(2,1)} async-done(((bf16[512,512]{1,0:T(8,128)(2,1)}), bf16[512,4096]{1,0:T(8,128)(2,1)}) %all-gather.2.cloned.1.call-update) | async-done | bytes 4194320 | tf_op jit(solution)/shard_map/all_gather | solution.py:95
  44.3 3.0 %convert_reduce_fusion = f32[512]{0:T(512)S(1)} fusion(bf16[512,4096]{1,0:T(8,128)(2,1)} %all-gather.2.cloned.1.call-done), kind=kLoop, calls=%fused_computation.4 | loop fusion | flops 4193792 | bytes 4196352 | tf_op jit(solution)/shard_map/reduce_sum | solution.py:13
  47.7 1.2 fusion.9
  49.0 6.6 %fusion.12 = f32[512,768]{0,1:T(8,128)S(1)} fusion(bf16[4096,768]{1,0:T(8,128)(2,1)} %param.16, bf16[512,4096]{1,0:T(8,128)(2,1)S(1)} %copy-done.1, f32[4096]{0:T(1024)S(1)} %copy-done.10, f32[4096]{0:T(1024)S(1)} %copy-done.11, f32[512]{0:T(512)S(1)} %add_rsqrt_fusion, f32[512]{0:T(512)S(1)} %broadcast_multiply_fusion), kind=kOutput, calls=%fused_computation.16 | convolution fusion | flops 3233808384 | bytes 12095488 | tf_op jit(solution)/shard_map/dot_general | solution.py:36
  56.3 0.9 fusion.137
  57.4 0.9 slice.78
  58.2 1.1 slice_negate_fusion
  59.4 1.2 copy.58
  60.7 0.8 slice.98
  63.6 2.1 %fusion.138 = f32[2,512]{1,0:T(2,128)S(1)} fusion(pred[512,512]{0,1:T(8,128)(4,1)} %copy.46, bf16[512,2,128]{2,0,1:T(8,128)(2,1)S(1)} %maximum_convert_fusion, bf16[512,2,96]{2,0,1:T(8,128)(2,1)} %slice.98, bf16[512,2,32]{2,0,1:T(8,128)(2,1)S(1)} %fusion.75), kind=kOutput, calls=%fused_computation.173 | convolution fusion | flops 136839680 | bytes 790528 | tf_op jit(solution)/shard_map/sub | solution.py:54
  65.8 2.3 %convolution_convert_fusion = bf16[2,128,512]{2,1,0:T(8,128)(2,1)S(1)} fusion(f32[2,512]{1,0:T(2,128)S(1)} %fusion.138, bf16[512,2,1,128]{0,3,1,2:T(8,128)(2,1)S(1)} %copy-done.7, pred[512,512]{0,1:T(8,128)(4,1)} %copy.46, bf16[512,2,128]{2,0,1:T(8,128)(2,1)S(1)} %maximum_convert_fusion, bf16[512,2,96]{2,0,1:T(8,128)(2,1)S(1)} %copy-done.9, ...), kind=kOutput, calls=%fused_computation.49 | convolution fusion | flops 271713792 | bytes 1314816 | tf_op jit(solution)/shard_map/hqk,khd->qhd/dot_general | solution.py:56
  68.1 23.6 %fusion.35 = f32[512,4096]{1,0:T(8,128)} fusion(bf16[1024,4096]{1,0:T(8,128)(2,1)} %param.19, bf16[4096,1024]{1,0:T(8,128)(2,1)} %param.18, bf16[512,4096]{1,0:T(8,128)(2,1)} %all-gather.2.cloned.1.call-done, f32[4096]{0:T(1024)S(1)} %copy-done.12, f32[4096]{0:T(1024)S(1)} %copy-done.13, f32[512]{0:T(512)S(1)} %add_rsqrt_fusion, ...), kind=kOutput, calls=%fused_computation.47 | convolution fusion | flops 8636596224 | bytes 29396992 | tf_op jit(solution)/shard_map/dot_general | solution.py:108
  91.7 6.6 %add_convert_fusion = bf16[512,4096]{1,0:T(8,128)(2,1)} fusion(f32[512,4096]{1,0:T(8,128)} %fusion.35, bf16[512,256]{0,1:T(8,128)(2,1)S(1)} %bitcast.45, bf16[256,4096]{1,0:T(8,128)(2,1)S(1)} %copy-done), kind=kOutput, calls=%fused_computation.14 | convolution fusion | flops 1077936128 | bytes 14942208 | tf_op jit(solution)/shard_map/dot_general | solution.py:108
  99.6 1.4 dynamic-update-slice
  101.0 16.5 %all-reduce = s32[16]{0:T(128)S(1)} all-reduce(s32[16]{0:T(128)S(1)} %dynamic-update-slice), channel_id=1, replica_groups=mesh['req'=16,'mlp'=8] {'req'}, use_global_device_ids=true, to_apply=%add | all-reduce | flops 16 | bytes 128
  118.6 2.4 %scatter_custom_fusion = s32[256]{0:T(256)S(1)} fusion(s32[512]{0:T(512)S(1)} %bitcast.47, s32[512]{0:T(512)S(1)} %iota.32, s32[]{:T(128)} %constant.46.clone.1), kind=kCustom, calls=%fused_computation.131 | custom fusion | bytes 1028 | tf_op jit(solution)/shard_map/scatter | solution.py:93
  121.9 1.1 copy.54
  123.0 3.6 %all-to-all-start = ((bf16[32,16,512]{2,0,1:T(8,128)(2,1)}), bf16[32,16,512]{2,0,1:T(8,128)(2,1)S(1)}, u32[]{:S(2)}, u32[]{:S(2)}) async-start(bf16[32,16,512]{2,0,1:T(8,128)(2,1)} %copy.54), calls=%async_computation.1 | async-start | bytes 1048576 | tf_op jit(solution)/shard_map/all_to_all | solution.py:99
  126.6 10.1 %all-to-all-done = bf16[32,16,512]{2,0,1:T(8,128)(2,1)S(1)} async-done(((bf16[32,16,512]{2,0,1:T(8,128)(2,1)}), bf16[32,16,512]{2,0,1:T(8,128)(2,1)S(1)}, u32[]{:S(2)}, u32[]{:S(2)}) %all-to-all-start) | async-done | bytes 524320 | tf_op jit(solution)/shard_map/all_to_all | solution.py:99
  136.7 1.2 gather_fusion
  138.7 2.2 %add_select_fusion = f32[512,512]{1,0:T(8,128)} fusion(bf16[512,512]{1,0:T(8,128)(2,1)} %reduce-scatter.2.cloned.1.call-done, bf16[512,512]{1,0:T(8,128)(2,1)S(1)} %copy-done.3, pred[512]{0:T(512)(128)(4,1)S(1)} %get-tuple-element.3), kind=kLoop, calls=%fused_computation.50 | loop fusion | flops 1048576 | bytes 2097664 | tf_op jit(solution)/shard_map/jit(_where)/select_n | solution.py:115
  (77 shorter events, 9.5 us)
Async XLA Ops:
  7.2 84.6 %copy-start = (bf16[256,4096]{1,0:T(8,128)(2,1)S(1)}, bf16[256,4096]{1,0:T(8,128)(2,1)}, u32[]{:S(2)}) copy-start(bf16[256,4096]{1,0:T(8,128)(2,1)} %param.17) | copy-start | bytes 6291460
  7.2 37.1 %all-gather.2.cloned.1.call-start = ((), (), s32[]{:S(2)}) async-start(), calls=%async_computation.2 | async-start | bytes 4718592 | tf_op jit(solution)/shard_map/all_gather | solution.py:95
  7.9 130.8 %reduce-scatter.2.cloned.1.call-start = ((), (), s32[]{:S(2)}) async-start(), calls=%async_computation.3 | async-start | bytes 4718592 | tf_op jit(solution)/shard_map/reduce_scatter | solution.py:111
  44.3 3.4 %copy-start.1 = (bf16[512,4096]{1,0:T(8,128)(2,1)S(1)}, bf16[512,4096]{1,0:T(8,128)(2,1)}, u32[]{:S(2)}) copy-start(bf16[512,4096]{1,0:T(8,128)(2,1)} %all-gather.2.cloned.1.call-done) | copy-start | bytes 12582916
  47.7 1.2 copy-start.10
  47.7 1.2 copy-start.11
  60.6 1.1 copy-start.2
  60.6 1.2 copy-start.4
  60.7 1.4 copy-start.5
  61.5 1.0 copy-start.6
  62.9 0.7 copy-start.8
  63.6 2.1 %copy-start.7 = (bf16[512,2,1,128]{0,3,1,2:T(8,128)(2,1)S(1)}, bf16[512,2,1,128]{0,3,1,2:T(8,128)(2,1)}, u32[]{:S(2)}) copy-start(bf16[512,2,1,128]{0,3,1,2:T(8,128)(2,1)} %fusion.76) | copy-start | bytes 786436
  63.6 2.1 %copy-start.9 = (bf16[512,2,96]{2,0,1:T(8,128)(2,1)S(1)}, bf16[512,2,96]{2,0,1:T(8,128)(2,1)}, u32[]{:S(2)}) copy-start(bf16[512,2,96]{2,0,1:T(8,128)(2,1)} %slice.98) | copy-start | bytes 589828
  65.7 2.3 %copy-start.12 = (f32[4096]{0:T(1024)S(1)}, f32[4096]{0:T(1024)}, u32[]{:S(2)}) copy-start(f32[4096]{0:T(1024)} %param.15) | copy-start | bytes 49156
  65.8 2.3 %copy-start.13 = (f32[4096]{0:T(1024)S(1)}, f32[4096]{0:T(1024)}, u32[]{:S(2)}) copy-start(f32[4096]{0:T(1024)} %param.14) | copy-start | bytes 49156
  98.4 0.7 copy-start.14
  123.0 13.7 %all-to-all-start = ((bf16[32,16,512]{2,0,1:T(8,128)(2,1)}), bf16[32,16,512]{2,0,1:T(8,128)(2,1)S(1)}, u32[]{:S(2)}, u32[]{:S(2)}) async-start(bf16[32,16,512]{2,0,1:T(8,128)(2,1)} %copy.54), calls=%async_computation.1 | async-start | bytes 1048576 | tf_op jit(solution)/shard_map/all_to_all | solution.py:99
  126.6 12.1 %copy-start.3 = (bf16[512,512]{1,0:T(8,128)(2,1)S(1)}, bf16[512,512]{1,0:T(8,128)(2,1)}, u32[]{:S(2)}) copy-start(bf16[512,512]{1,0:T(8,128)(2,1)} %param.10) | copy-start | bytes 1572868
Sparse Core Ops, SparseCore 0:
  9.7 34.5 all-gather.1
  98.5 38.3 reduce-scatter.1
where the time goes:
time: 148 us
  waiting for transfers between devices  42.5 us (29%)
  matrix products  41.2 us (28%)
  local copies, waits for them, and re-layouts  17.2 us (12%)
  blocking collectives  16.5 us (11%)
  between operations  14.4 us (10%)
  other arithmetic  12.3 us (8%)
  starting transfers between devices  3.65 us (2%)
    all_gather x1, waiting for transfers between devices, body(): full_rows = lax.all_gather(activations, 'mlp', axis=1, tiled=True)  31.7 us
    dot_general x1, matrix products, body(): jnp.dot(hidden, proj_weight, preferred_element_type=jnp.float32)  23.6 us
    unnamed x1, blocking collectives  16.5 us
    all_to_all x1, waiting for transfers between devices, body(): lax.all_to_all(key_value, 'req', split_axis=1, concat_axis=0, tiled=True)  10.1 us
    dot_general x1, matrix products, body(): jnp.dot(context, dense_weight, preferred_element_type=jnp.float32)  6.64 us
    dot_general x1, matrix products, attend(): jnp.dot(normed, qkv_weight, preferred_element_type=jnp.float32)  6.56 us
    unnamed x35, local copies, waits for them, and re-layouts  5.81 us
    all_to_all x1, starting transfers between devices, body(): lax.all_to_all(key_value, 'req', split_axis=1, concat_axis=0, tiled=True)  3.57 us
  transfers between devices with their start and end apart: 3, of which 2 were waited for; matrix products, arithmetic and copies ran while one was open for 9% of the time, Pallas kernels for 0%

commit v1 on v0

--- a/solution.py
+++ b/solution.py
@@ -92,7 +92,9 @@
         .at[target]
         .set(jnp.arange(groups * per_peer, dtype=jnp.int32), mode="drop")
     )
-    full_rows = lax.all_gather(activations, "mlp", axis=1, tiled=True)
+    full_rows = jnp.concatenate(
+        lax.all_to_all(jnp.stack([activations] * lax.axis_size("mlp")), "mlp", 0, 0), axis=1
+    )
     normed = layer_norm(full_rows, attn_norm_gain, attn_norm_bias)
     context, key_rows, value_rows = attend(normed, slot_segment, qkv_weight)
     key_value = jnp.concatenate([key_rows, value_rows], axis=1).reshape(per_peer, groups, -1)

time: 148 us -> 174 us (1.18)
  local copies, waits for them, and re-layouts: 17.2 us -> 31.5 us
  waiting for transfers between devices: 42.5 us -> 49.3 us
  starting transfers between devices: 3.65 us -> 8.33 us
  matrix products: 41.2 us -> 38 us
    all_to_all x0 -> x1, waiting for transfers between devices: none -> 39.3 us  [body(): lax.all_to_all(jnp.stack([activations] * lax.axis_size('mlp')), 'mlp', 0, 0)]
    all_gather x1 -> x0, waiting for transfers between devices: 31.7 us -> none  [body(): full_rows = lax.all_gather(activations, 'mlp', axis=1, tiled=True)]
    unnamed x35 -> x30, local copies, waits for them, and re-layouts: 5.81 us -> 13.8 us
    all_to_all x0 -> x1, local copies, waits for them, and re-layouts: none -> 6.52 us  [body(): lax.all_to_all(jnp.stack([activations] * lax.axis_size('mlp')), 'mlp', 0, 0)]
    all_to_all x0 -> x1, starting transfers between devices: none -> 4.71 us  [body(): lax.all_to_all(jnp.stack([activations] * lax.axis_size('mlp')), 'mlp', 0, 0)]
    convert_element_type x0 -> x2, other arithmetic: none -> 4.64 us  [layer_norm(): (centered * lax.rsqrt(variance + 1e-05) * gain_vec + bias_vec).astype(jnp...]
    another operation x1 -> x2, local copies, waits for them, and re-layouts: 0.12 us -> 3.7 us  [the longest x1 3.59 us: body(): jnp.stack([activations] * lax.axis_size('mlp'))]
    dot_general x1, matrix products: 6.56 us -> 3.4 us  [attend(): jnp.dot(normed, qkv_weight, preferred_element_type=jnp.float32)]
  transfers between devices with their start and end apart: 3 -> 3, of which waited for: 2 -> 2; matrix products, arithmetic and copies ran while one was open for 9% -> 12% of each run, Pallas kernels for 0% -> 0%
where the time goes in v1:
time: 174 us; the launch traced here: 173 us
  waiting for transfers between devices  49.3 us (28%)
  matrix products  38 us (22%)
  local copies, waits for them, and re-layouts  31.5 us (18%)
  blocking collectives  17.8 us (10%)
  between operations  14.3 us (8%)
  other arithmetic  13.6 us (8%)
  starting transfers between devices  8.33 us (5%)
    all_to_all x1, waiting for transfers between devices, body(): lax.all_to_all(jnp.stack([activations] * lax.axis_size('mlp')), 'mlp', 0, 0)  39.3 us
    dot_general x1, matrix products, body(): jnp.dot(hidden, proj_weight, preferred_element_type=jnp.float32)  23.4 us
    unnamed x1, blocking collectives  17.8 us
    unnamed x30, local copies, waits for them, and re-layouts  13.8 us
    all_to_all x1, waiting for transfers between devices, body(): lax.all_to_all(key_value, 'req', split_axis=1, concat_axis=0, tiled=True)  10.1 us
    dot_general x1, matrix products, body(): jnp.dot(context, dense_weight, preferred_element_type=jnp.float32)  6.64 us
    all_to_all x1, local copies, waits for them, and re-layouts, body(): lax.all_to_all(jnp.stack([activations] * lax.axis_size('mlp')), 'mlp', 0, 0)  6.52 us
    all_to_all x1, starting transfers between devices, body(): lax.all_to_all(jnp.stack([activations] * lax.axis_size('mlp')), 'mlp', 0, 0)  4.71 us
  transfers between devices with their start and end apart: 3, of which 2 were waited for; matrix products, arithmetic and copies ran while one was open for 12% of the time, Pallas kernels for 0%

profile of v1, /device:TPU:0, one launch (start us, length us, event | category | flops | bytes accessed | tf_op | source)
XLA Modules:
  0.0 172.9 jit_solution(12294881369838541176)
XLA Ops:
  7.2 3.6 %stack.8 = bf16[8,512,512]{2,1,0:T(8,128)(2,1)} broadcast(bf16[512,512]{1,0:T(8,128)(2,1)} %param.10), dimensions={1,2} | broadcast | bytes 4718592 | tf_op jit(solution)/shard_map/stack | solution.py:96
  10.8 4.7 %all-to-all-start = ((bf16[8,512,512]{2,1,0:T(8,128)(2,1)}), bf16[8,512,512]{2,1,0:T(8,128)(2,1)}, u32[]{:S(2)}, u32[]{:S(2)}) async-start(bf16[8,512,512]{2,1,0:T(8,128)(2,1)} %stack.8), calls=%async_computation | async-start | bytes 8388608 | tf_op jit(solution)/shard_map/all_to_all | solution.py:96
  15.6 8.8 %copy.38 = bf16[4096,768]{0,1:T(8,128)(2,1)} copy(bf16[4096,768]{1,0:T(8,128)(2,1)} %param.16) | data formatting | bytes 12582912 | tf_op args[6]
  25.9 39.3 %all-to-all-done = bf16[8,512,512]{2,1,0:T(8,128)(2,1)} async-done(((bf16[8,512,512]{2,1,0:T(8,128)(2,1)}), bf16[8,512,512]{2,1,0:T(8,128)(2,1)}, u32[]{:S(2)}, u32[]{:S(2)}) %all-to-all-start) | async-done | bytes 4194336 | tf_op jit(solution)/shard_map/all_to_all | solution.py:96
  65.2 6.5 %copy.37 = bf16[8,512,512]{1,2,0:T(8,128)(2,1)} copy(bf16[8,512,512]{2,1,0:T(8,128)(2,1)} %all-to-all-done) | data formatting | bytes 8388608 | tf_op jit(solution)/shard_map/all_to_all | solution.py:96
  71.7 3.0 %convert_reduce_fusion = f32[512]{0:T(512)S(1)} fusion(bf16[8,512,512]{1,2,0:T(8,128)(2,1)} %copy.37), kind=kLoop, calls=%fused_computation.11 | loop fusion | flops 4193792 | bytes 4196352 | tf_op jit(solution)/shard_map/reduce_sum | solution.py:13
  75.1 1.2 multiply_reduce_fusion
  76.3 1.8 %add_convert_fusion = bf16[8,512,512]{1,2,0:T(8,128)(2,1)S(1)} fusion(bf16[8,512,512]{1,2,0:T(8,128)(2,1)S(1)} %copy-done.1, f32[8,512]{1,0:T(8,128)S(1)} %add.72, f32[8,512]{1,0:T(8,128)S(1)} %mul.121, f32[512]{0:T(512)S(1)} %add_rsqrt_fusion, f32[512]{0:T(512)S(1)} %broadcast_multiply_fusion), kind=kLoop, calls=%fused_computation.8 | loop fusion | flops 12582912 | bytes 8425472 | tf_op jit(solution)/shard_map/convert_element_type | solution.py:16
  78.2 3.4 %fusion.110 = f32[512,2,3,128]{0,3,2,1:T(8,128)S(1)} fusion(bf16[512,4096,1,1]{0,1,3,2:T(8,128)(2,1)S(1)} %bitcast.58, bf16[2,3,128,4096]{3,2,1,0:T(8,128)(2,1)S(1)} %bitcast.57), kind=kOutput, calls=%fused_computation.159 | convolution fusion | flops 3221225472 | bytes 12058624 | tf_op jit(solution)/shard_map/dot_general | solution.py:36
  81.9 1.0 copy-done.4
  82.9 2.4 %fusion.104 = (f32[2,512]{1,0:T(2,128)S(1)}, f32[2,512,512]{1,2,0:T(8,128)}) fusion(pred[512,512]{0,1:T(8,128)(4,1)S(1)} %copy.40, bf16[512,2,96]{0,2,1:T(8,128)(2,1)S(1)} %slice.99, bf16[512,2,32]{0,2,1:T(8,128)(2,1)S(1)} %fusion.64, bf16[512,2,96]{0,2,1:T(8,128)(2,1)S(1)} %slice.78, bf16[512,2,32]{0,2,1:T(8,128)(2,1)S(1)} %fusion.62), kind=kOutput, calls=%fused_computation.156 | convolution fusion | flops 137363968 | bytes 2887680 | tf_op jit(solution)/shard_map/sub | solution.py:54
  85.2 2.2 %convolution_convert_fusion = bf16[2,128,512]{2,1,0:T(8,128)(2,1)S(1)} fusion(f32[2,512,512]{1,2,0:T(8,128)} %get-tuple-element.16, f32[2,512]{1,0:T(2,128)S(1)} %get-tuple-element.15, f32[512,2,3,128]{0,3,2,1:T(8,128)} %copy-done.4), kind=kOutput, calls=%fused_computation.35 | convolution fusion | flops 135397376 | bytes 2625536 | tf_op jit(solution)/shard_map/hqk,khd->qhd/dot_general | solution.py:56
  88.2 2.9 %fusion.4 = bf16[512,4096]{0,1:T(8,128)(2,1)} fusion(bf16[8,512,512]{1,2,0:T(8,128)(2,1)S(1)} %copy-done.2, f32[4096]{0:T(1024)S(1)} %copy-done.6, f32[4096]{0:T(1024)S(1)} %copy-done.7, f32[512]{0:T(512)S(1)} %add_rsqrt_fusion, f32[512]{0:T(512)S(1)} %broadcast_multiply_fusion), kind=kLoop, calls=%fused_computation.7 | loop fusion | flops 12582912 | bytes 8425472 | tf_op jit(solution)/shard_map/convert_element_type | solution.py:16
  91.1 23.4 %fusion.16 = f32[512,4096]{1,0:T(8,128)} fusion(bf16[1024,4096]{1,0:T(8,128)(2,1)} %param.19, bf16[512,4096]{0,1:T(8,128)(2,1)} %fusion.4, bf16[4096,1024]{1,0:T(8,128)(2,1)} %param.18), kind=kOutput, calls=%fused_computation.36 | convolution fusion | flops 8624013312 | bytes 29360128 | tf_op jit(solution)/shard_map/dot_general | solution.py:110
  114.5 6.6 %add_convert_fusion.1 = bf16[512,4096]{1,0:T(8,128)(2,1)} fusion(f32[512,4096]{1,0:T(8,128)} %fusion.16, bf16[512,256]{0,1:T(8,128)(2,1)S(1)} %bitcast.59, bf16[256,4096]{1,0:T(8,128)(2,1)S(1)} %copy-done), kind=kOutput, calls=%fused_computation.9 | convolution fusion | flops 1077936128 | bytes 14942208 | tf_op jit(solution)/shard_map/dot_general | solution.py:110
  122.4 1.4 dynamic-update-slice
  123.8 17.8 %all-reduce = s32[16]{0:T(128)S(1)} all-reduce(s32[16]{0:T(128)S(1)} %dynamic-update-slice), channel_id=1, replica_groups=mesh['req'=16,'mlp'=8] {'req'}, use_global_device_ids=true, to_apply=%add | all-reduce | flops 16 | bytes 128
  142.7 2.4 %scatter_custom_fusion = s32[256]{0:T(256)S(1)} fusion(s32[512]{0:T(512)S(1)} %bitcast.61, s32[512]{0:T(512)S(1)} %iota.32, s32[]{:T(128)} %constant.46.clone.1), kind=kCustom, calls=%fused_computation.119 | custom fusion | bytes 1028 | tf_op jit(solution)/shard_map/scatter | solution.py:93
  145.2 1.1 slice.98
  147.1 1.1 copy.47
  148.2 3.6 %all-to-all-start.1 = ((bf16[32,16,512]{2,0,1:T(8,128)(2,1)}), bf16[32,16,512]{2,0,1:T(8,128)(2,1)S(1)}, u32[]{:S(2)}, u32[]{:S(2)}) async-start(bf16[32,16,512]{2,0,1:T(8,128)(2,1)} %copy.47), calls=%async_computation.2 | async-start | bytes 1048576 | tf_op jit(solution)/shard_map/all_to_all | solution.py:101
  151.8 10.1 %all-to-all-done.1 = bf16[32,16,512]{2,0,1:T(8,128)(2,1)S(1)} async-done(((bf16[32,16,512]{2,0,1:T(8,128)(2,1)}), bf16[32,16,512]{2,0,1:T(8,128)(2,1)S(1)}, u32[]{:S(2)}, u32[]{:S(2)}) %all-to-all-start.1) | async-done | bytes 524320 | tf_op jit(solution)/shard_map/all_to_all | solution.py:101
  161.8 1.2 gather_fusion
  163.9 2.2 %add_select_fusion = f32[512,512]{1,0:T(8,128)} fusion(bf16[512,512]{1,0:T(8,128)(2,1)} %reduce-scatter.2.cloned.1.call-done, bf16[512,512]{1,0:T(8,128)(2,1)S(1)} %copy-done.3, pred[512]{0:T(512)(128)(4,1)S(1)} %get-tuple-element.3), kind=kLoop, calls=%fused_computation.37 | loop fusion | flops 1048576 | bytes 2097664 | tf_op jit(solution)/shard_map/jit(_where)/select_n | solution.py:117
  (75 shorter events, 7.1 us)
Async XLA Ops:
  7.2 107.3 %copy-start = (bf16[256,4096]{1,0:T(8,128)(2,1)S(1)}, bf16[256,4096]{1,0:T(8,128)(2,1)}, u32[]{:S(2)}) copy-start(bf16[256,4096]{1,0:T(8,128)(2,1)} %param.17) | copy-start | bytes 6291460
  10.8 4.8 %copy-start.8 = (f32[4096]{0:T(1024)S(1)}, f32[4096]{0:T(1024)}, u32[]{:S(2)}) copy-start(f32[4096]{0:T(1024)} %param.13) | copy-start | bytes 49156
  10.8 4.8 %copy-start.9 = (f32[4096]{0:T(1024)S(1)}, f32[4096]{0:T(1024)}, u32[]{:S(2)}) copy-start(f32[4096]{0:T(1024)} %param.12) | copy-start | bytes 49156
  10.8 54.4 %all-to-all-start = ((bf16[8,512,512]{2,1,0:T(8,128)(2,1)}), bf16[8,512,512]{2,1,0:T(8,128)(2,1)}, u32[]{:S(2)}, u32[]{:S(2)}) async-start(bf16[8,512,512]{2,1,0:T(8,128)(2,1)} %stack.8), calls=%async_computation | async-start | bytes 8388608 | tf_op jit(solution)/shard_map/all_to_all | solution.py:96
  15.5 148.4 %reduce-scatter.2.cloned.1.call-start = ((), (), s32[]{:S(2)}) async-start(), calls=%async_computation.3 | async-start | bytes 4718592 | tf_op jit(solution)/shard_map/reduce_scatter | solution.py:113
  15.6 8.8 %copy-start.5 = (s32[512]{0:T(512)S(1)}, s32[512]{0:T(512)}, u32[]{:S(2)}) copy-start(s32[512]{0:T(512)} %param.11) | copy-start | bytes 6148
  71.7 3.4 %copy-start.1 = (bf16[8,512,512]{1,2,0:T(8,128)(2,1)S(1)}, bf16[8,512,512]{1,2,0:T(8,128)(2,1)}, u32[]{:S(2)}) copy-start(bf16[8,512,512]{1,2,0:T(8,128)(2,1)} %copy.37) | copy-start | bytes 12582916
  75.1 2.9 %slice-start = ((s8[6291456]{0:T(1024)(128)(4,1)}), s8[4194304]{0:T(1024)(128)(4,1)S(1)}, s32[]{:S(2)}) async-start(s8[6291456]{0:T(1024)(128)(4,1)} %bitcast.55), calls=%async_computation.4 | async-start | bytes 8388608
  76.3 1.9 %slice-start.1 = ((s8[6291456]{0:T(1024)(128)(4,1)}), s8[2097152]{0:T(1024)(128)(4,1)S(1)}, s32[]{:S(2)}) async-start(s8[6291456]{0:T(1024)(128)(4,1)} %bitcast.55), calls=%async_computation.5 | async-start | bytes 4194304
  81.6 1.2 copy-start.4
  85.2 3.0 %copy-start.2 = (bf16[8,512,512]{1,2,0:T(8,128)(2,1)S(1)}, bf16[8,512,512]{1,2,0:T(8,128)(2,1)}, u32[]{:S(2)}) copy-start(bf16[8,512,512]{1,2,0:T(8,128)(2,1)} %copy.37) | copy-start | bytes 12582916
  85.2 3.0 %copy-start.6 = (f32[4096]{0:T(1024)S(1)}, f32[4096]{0:T(1024)}, u32[]{:S(2)}) copy-start(f32[4096]{0:T(1024)} %param.15) | copy-start | bytes 49156
  85.2 3.0 %copy-start.7 = (f32[4096]{0:T(1024)S(1)}, f32[4096]{0:T(1024)}, u32[]{:S(2)}) copy-start(f32[4096]{0:T(1024)} %param.14) | copy-start | bytes 49156
  121.2 0.7 copy-start.10
  148.2 13.7 %all-to-all-start.1 = ((bf16[32,16,512]{2,0,1:T(8,128)(2,1)}), bf16[32,16,512]{2,0,1:T(8,128)(2,1)S(1)}, u32[]{:S(2)}, u32[]{:S(2)}) async-start(bf16[32,16,512]{2,0,1:T(8,128)(2,1)} %copy.47), calls=%async_computation.2 | async-start | bytes 1048576 | tf_op jit(solution)/shard_map/all_to_all | solution.py:101
  151.7 12.1 %copy-start.3 = (bf16[512,512]{1,0:T(8,128)(2,1)S(1)}, bf16[512,512]{1,0:T(8,128)(2,1)}, u32[]{:S(2)}) copy-start(bf16[512,512]{1,0:T(8,128)(2,1)} %param.10) | copy-start | bytes 1572868
Sparse Core Ops, SparseCore 0:
  121.3 38.4 reduce-scatter.1
